TPU v7x, 256 devices: a whole 4x4x8 slice. The times are simulated.
256 devices in a mesh: seq: 32 (over y_lo, z, core), head: 8 (over y_hi, x).
Axes of the slice: x: 4, y: 4 (y_hi: 2, y_lo: 2; y = y_hi * 2 + y_lo), z: 8, core: 2. Of those that a mesh axis runs over, the one named last changes fastest.
Arguments:
- inputs: bfloat16 [16384, 5376], P('seq'), may hold values from -6 to 6
- queries: bfloat16 [16384, 4096], P('seq', 'head'), may hold values from -6 to 6
- key_matrix: bfloat16 [5376, 2048], P('seq', 'head'), may hold values from -0.078125 to 0.078125
- value_matrix: bfloat16 [5376, 2048], P('seq', 'head'), may hold values from -0.078125 to 0.078125
- readout: bfloat16 [4096, 512], P('head'), may hold values from -6 to 6
- token_mask: int32 [16384], P('seq'), may hold values 0 or 1
- targets: int32 [16384], P('seq'), may hold values from 0 to 511
Outputs:
- query_grad: float32 [16384, 4096], P('seq', 'head')
- input_grad: float32 [16384, 5376], P('seq', 'head')
All inputs are finite; a program needn't handle non-finite values. No bound on the sum of `token_mask` on one device may be relied on, other than what follows from the above.
Results may differ from a plain program's by a relative error of at most 0.028.
Values may be sent and summed in bfloat16 or wider, within the bound.
No kernel may reach another device: no remote copies, remote signals or barrier semaphores. Data moves between devices by JAX's collectives and lax.ppermute only.
A program may use at most 128 MiB of HBM per device.

v0:
```python
import jax
import jax.numpy as jnp
from jax import lax
from jax.sharding import PartitionSpec as P

HEAD_SIZE = 128
WINDOW_KEYS = 1024
norm_eps = 1e-06
softcap = 30.0
score_scale = 168.0 ** (-0.5)


def passed_along(value, axis, steps):
    count = lax.axis_size(axis)
    leading, last = (max(0, -steps), min(count, count - steps))
    return lax.ppermute(value, axis, [(source, source + steps) for source in range(leading, last)])


def normalized_rows(value_rows):
    inverse = lax.rsqrt(jnp.mean(value_rows * value_rows, axis=-1, keepdims=True) + norm_eps)
    return (value_rows * inverse, inverse)


def unit_norm_backward(unit, inverse, upstream):
    return inverse * (upstream - unit * jnp.mean(unit * upstream, axis=-1, keepdims=True))


def shards(inputs, queries, key_matrix, value_matrix, readout, token_mask, targets):
    tokens = inputs.shape[0]
    kv_width = key_matrix.shape[1]
    kv_heads = kv_width // HEAD_SIZE
    q_heads = queries.shape[1] // HEAD_SIZE
    query_groups = q_heads // kv_heads
    reach = WINDOW_KEYS // tokens
    span = (reach + 1) * tokens
    stacked = jnp.concatenate([key_matrix, value_matrix], axis=1)
    full_weight = lax.all_gather(stacked, "seq", axis=0, tiled=True)
    projected = jnp.dot(inputs, full_weight, preferred_element_type=jnp.float32)
    key_unscaled = projected[:, :kv_width].reshape(tokens, kv_heads, HEAD_SIZE)
    value_rows = projected[:, kv_width:].astype(jnp.bfloat16).reshape(tokens, kv_heads, HEAD_SIZE)
    key_unit_rows, key_inverse_norm = normalized_rows(key_unscaled)
    key_normalized_rows = key_unit_rows.astype(jnp.bfloat16)
    query_unit_rows, query_inverse_norm = normalized_rows(
        queries.astype(jnp.float32).reshape(tokens, kv_heads, query_groups, HEAD_SIZE)
    )
    query_hat = query_unit_rows.astype(jnp.bfloat16)
    paired = jnp.concatenate([key_normalized_rows, value_rows], axis=-1)
    earlier = [passed_along(paired, "seq", offset) for offset in range(reach, 0, -1)]
    window_kv = jnp.concatenate(earlier + [paired], axis=0)
    key_block = window_kv[..., :HEAD_SIZE]
    value_block = window_kv[..., HEAD_SIZE:]
    first = lax.axis_index("seq") * tokens
    query_pos = first + jnp.arange(tokens, dtype=jnp.int32)
    key_pos = first - reach * tokens + jnp.arange(span, dtype=jnp.int32)
    distance = query_pos[:, None] - key_pos[None, :]
    visible = (distance >= 0) & (distance < WINDOW_KEYS) & (key_pos[None, :] >= 0)
    scores = (
        jnp.einsum("qkgd,jkd->kgqj", query_hat, key_block, preferred_element_type=jnp.float32)
        * score_scale
    )
    raised = jnp.where(visible, jnp.exp(scores), 0.0)
    attn = (raised / jnp.sum(raised, axis=-1, keepdims=True)).astype(jnp.bfloat16)
    attended = jnp.einsum(
        "kgqj,jkd->qkgd", attn, value_block, preferred_element_type=jnp.float32
    ).astype(jnp.bfloat16)
    flat = attended.reshape(tokens, q_heads * HEAD_SIZE)
    partial_value = jnp.dot(flat, readout, preferred_element_type=jnp.float32)
    logits = lax.psum(partial_value.astype(jnp.bfloat16), "head").astype(jnp.float32)
    capped = softcap * jnp.tanh(logits / softcap)
    expo = jnp.exp(capped)
    probs = expo / jnp.sum(expo, axis=-1, keepdims=True)
    onehot = (targets[:, None] == jnp.arange(logits.shape[1], dtype=jnp.int32)[None, :]).astype(
        jnp.float32
    )
    chosen = token_mask.astype(jnp.float32)[:, None]
    dlogits = (chosen * (probs - onehot) * (1.0 - (capped / softcap) ** 2)).astype(jnp.bfloat16)
    attended_grad = lax.dot_general(
        dlogits, readout, (((1,), (1,)), ((), ())), preferred_element_type=jnp.float32
    )
    attended_grad = attended_grad.astype(jnp.bfloat16).reshape(
        tokens, kv_heads, query_groups, HEAD_SIZE
    )
    d_weights = jnp.einsum(
        "qkgd,jkd->kgqj", attended_grad, value_block, preferred_element_type=jnp.float32
    )
    attn_f = attn.astype(jnp.float32)
    d_scores = (attn_f * (d_weights - jnp.sum(attn_f * d_weights, axis=-1, keepdims=True))).astype(
        jnp.bfloat16
    )
    d_query_hat = (
        jnp.einsum("kgqj,jkd->qkgd", d_scores, key_block, preferred_element_type=jnp.float32)
        * score_scale
    )
    d_key_hat = (
        jnp.einsum("kgqj,qkgd->jkd", d_scores, query_hat, preferred_element_type=jnp.float32)
        * score_scale
    )
    d_value = jnp.einsum("kgqj,qkgd->jkd", attn, attended_grad, preferred_element_type=jnp.float32)
    query_grad = unit_norm_backward(query_unit_rows, query_inverse_norm, d_query_hat).reshape(
        tokens, q_heads * HEAD_SIZE
    )
    pieces_all = jnp.concatenate([d_key_hat, d_value], axis=-1)
    pieces = [
        pieces_all[slot_index * tokens : (slot_index + 1) * tokens]
        for slot_index in range(reach + 1)
    ]
    total = pieces[reach]
    for offset in range(1, reach + 1):
        total = total + passed_along(
            pieces[reach - offset].astype(jnp.bfloat16), "seq", -offset
        ).astype(jnp.float32)
    key_weight_gradient = (
        unit_norm_backward(key_unit_rows, key_inverse_norm, total[..., :HEAD_SIZE])
        .astype(jnp.bfloat16)
        .reshape(tokens, kv_width)
    )
    value_weight_gradient = total[..., HEAD_SIZE:].astype(jnp.bfloat16).reshape(tokens, kv_width)
    both_grad = jnp.concatenate([key_weight_gradient, value_weight_gradient], axis=1)
    partial_grad = lax.dot_general(
        both_grad, full_weight, (((1,), (1,)), ((), ())), preferred_element_type=jnp.float32
    )
    input_grad = lax.psum_scatter(
        partial_grad.astype(jnp.bfloat16), "head", scatter_dimension=1, tiled=True
    ).astype(jnp.float32)
    return (query_grad, input_grad)


def solution(mesh):
    in_specs = (
        P("seq", None),
        P("seq", "head"),
        P("seq", "head"),
        P("seq", "head"),
        P("head", None),
        P("seq"),
        P("seq"),
    )
    out_specs = (P("seq", "head"), P("seq", "head"))
    return jax.shard_map(shards, mesh=mesh, in_specs=in_specs, out_specs=out_specs, check_vma=False)
```

profile of v0, /device:TPU:1, one launch (start us, length us, event | category | flops | bytes accessed | tf_op | source)
XLA Modules:
  0.0 374.4 jit_solution(5601554933877116850)
XLA Ops:
  7.2 1.7 pad_maximum_fusion.2
  9.0 1.3 copy.23
  10.4 72.4 %all-gather.2.cloned.1.call-done = bf16[5376,512]{1,0:T(8,128)(2,1)} async-done(((bf16[168,512]{1,0:T(8,128)(2,1)}), bf16[5376,512]{1,0:T(8,128)(2,1)}) %all-gather.2.cloned.1.call-update) | async-done | bytes 5505040 | tf_op jit(solution)/shard_map/all_gather | solution.py:37
  82.8 6.8 %convolution_bitcast_fusion.2 = f32[512,512]{0,1:T(8,128)S(1)} fusion(bf16[5376,512]{1,0:T(8,128)(2,1)} %all-gather.2.cloned.1.call-done, bf16[512,5376]{1,0:T(8,128)(2,1)} %param.7), kind=kOutput, calls=%fused_computation.24 | convolution fusion | flops 2818572288 | bytes 12058624 | tf_op jit(solution)/shard_map/dot_general | solution.py:38
  90.4 2.4 collective-permute-start.1
  92.8 3.8 %collective-permute-start = (bf16[512,2,256]{2,0,1:T(8,128)(2,1)S(1)}, bf16[512,2,256]{2,0,1:T(8,128)(2,1)S(1)}, u32[]{:S(2)}, u32[]{:S(2)}) collective-permute-start(bf16[512,2,256]{2,0,1:T(8,128)(2,1)S(1)} %pad_maximum_fusion.1), channel_id=1, source_target_pairs={{0,16},{8,24},{16,32},{24,40},{32,48},{40,56},{48,64},{56,72},{64,... | collective-permute-start | bytes 1572872 | tf_op jit(solution)/shard_map/ppermute | solution.py:16
  96.7 1.2 fusion.5
  97.9 3.9 %collective-permute-done.1 = bf16[512,2,256]{2,0,1:T(8,128)(2,1)S(1)} collective-permute-done((bf16[512,2,256]{2,0,1:T(8,128)(2,1)S(1)}, bf16[512,2,256]{2,0,1:T(8,128)(2,1)S(1)}, u32[]{:S(2)}, u32[]{:S(2)}) %collective-permute-start.1) | collective-permute-done | bytes 524320 | tf_op jit(solution)/shard_map/ppermute | solution.py:16
  101.8 8.3 %collective-permute-done = bf16[512,2,256]{2,0,1:T(8,128)(2,1)S(1)} collective-permute-done((bf16[512,2,256]{2,0,1:T(8,128)(2,1)S(1)}, bf16[512,2,256]{2,0,1:T(8,128)(2,1)S(1)}, u32[]{:S(2)}, u32[]{:S(2)}) %collective-permute-start) | collective-permute-done | bytes 524320 | tf_op jit(solution)/shard_map/ppermute | solution.py:16
  110.3 3.3 fusion.2
  113.6 2.7 divide_convert_fusion
  116.3 1.8 copy-done.5
  118.1 2.6 copy-done.2
  120.7 1.1 convolution_convert_fusion.3
  121.8 1.3 convolution_convert_fusion.2
  123.3 87.0 %all-reduce.2.cloned.1.call-done = bf16[512,512]{1,0:T(8,128)(2,1)} async-done(((bf16[512,512]{1,0:T(8,128)(2,1)}), bf16[512,512]{1,0:T(8,128)(2,1)}) %all-reduce.2.cloned.1.call-update) | async-done | bytes 524304 | tf_op jit(solution)/shard_map/psum | solution.py:68
  210.3 1.6 fusion.12
  211.9 2.3 convolution_convert_fusion.1
  214.2 1.8 convolution_bitcast_fusion
  216.1 6.9 %fusion = (f32[2,2,512]{2,1,0:T(2,128)S(1)}, f32[2,1536,512,2]{2,1,3,0:T(8,128)}) fusion(bf16[2,2,512,1536]{2,3,1,0:T(8,128)(2,1)S(1)} %copy-done.3, bf16[512,2,2,128]{0,3,2,1:T(8,128)(2,1)S(1)} %bitcast.87, bf16[1536,2,256]{2,0,1:T(8,128)(2,1)S(1)} %maximum_maximum_fusion), kind=kOutput, calls=%fused_computation.2 | convolution fusion | flops 814741504 | bytes 20193280 | tf_op jit(solution)/shard_map/qkgd,jkd->kgqj/dot_general | solution.py:83
  223.0 6.9 %fusion.1 = bf16[2,2,512,1536]{2,3,1,0:T(8,128)(2,1)S(1)} fusion(f32[2,1536,512,2]{2,1,3,0:T(8,128)} %get-tuple-element.11, f32[2,2,512]{2,1,0:T(2,128)S(1)} %get-tuple-element.10, f32[2,2,512]{2,1,0:T(2,128)S(1)} %get-tuple-element.8, f32[2,1536,512,2]{2,1,3,0:T(8,128)S(1)} %bitcast.85, pred[512,1536]{0,1:T(8,128)(4,1)S(1)} %copy-done.9), kind=kLoop, calls=%fused_computation.3 | loop fusion | flops 25165824 | bytes 32260096 | tf_op jit(solution)/shard_map/convert_element_type | solution.py:87
  229.9 1.8 fusion.7
  232.8 8.3 %collective-permute-start.2 = (bf16[512,2,256]{2,0,1:T(8,128)(2,1)S(1)}, bf16[512,2,256]{2,0,1:T(8,128)(2,1)S(1)}, u32[]{:S(2)}, u32[]{:S(2)}) collective-permute-start(bf16[512,2,256]{2,0,1:T(8,128)(2,1)S(1)} %get-tuple-element.6), channel_id=1, source_target_pairs={{8,0},{16,8},{24,16},{32,24},{40,32},{48,40},{56,48},{64,56},{72,6... | collective-permute-start | bytes 1572872 | tf_op jit(solution)/shard_map/ppermute | solution.py:16
  241.1 1.3 collective-permute-start.3
  242.4 10.4 %collective-permute-done.2 = bf16[512,2,256]{2,0,1:T(8,128)(2,1)S(1)} collective-permute-done((bf16[512,2,256]{2,0,1:T(8,128)(2,1)S(1)}, bf16[512,2,256]{2,0,1:T(8,128)(2,1)S(1)}, u32[]{:S(2)}, u32[]{:S(2)}) %collective-permute-start.2) | collective-permute-done | bytes 524320 | tf_op jit(solution)/shard_map/ppermute | solution.py:16
  252.8 4.1 %collective-permute-done.3 = bf16[512,2,256]{2,0,1:T(8,128)(2,1)S(1)} collective-permute-done((bf16[512,2,256]{2,0,1:T(8,128)(2,1)S(1)}, bf16[512,2,256]{2,0,1:T(8,128)(2,1)S(1)}, u32[]{:S(2)}, u32[]{:S(2)}) %collective-permute-start.3) | collective-permute-done | bytes 524320 | tf_op jit(solution)/shard_map/ppermute | solution.py:16
  258.6 1.1 copy.37
  259.8 7.4 %convolution_convert_fusion = bf16[512,5376]{0,1:T(8,128)(2,1)} fusion(bf16[5376,512]{1,0:T(8,128)(2,1)} %all-gather.2.cloned.1.call-done, bf16[512,256]{0,1:T(8,128)(2,1)S(1)} %bitcast.92, bf16[512,256]{0,1:T(8,128)(2,1)S(1)} %bitcast.93), kind=kOutput, calls=%fused_computation.8 | convolution fusion | flops 2822373376 | bytes 11534336 | tf_op jit(solution)/shard_map/dot_general | solution.py:119
  267.3 3.9 %multiply_reduce_fusion = (f32[512,2,2]{0,2,1:T(2,128)S(1)}, f32[512,2,2,128]{0,3,2,1:T(8,128)S(1)}) fusion(f32[512,512]{0,1:T(8,128)S(1)} %copy.23, f32[512,2,2]{0,2,1:T(2,128)S(1)} %add_rsqrt_fusion, bf16[2,2,512,1536]{2,3,1,0:T(8,128)(2,1)} %copy-done.4, bf16[1536,2,256]{2,0,1:T(8,128)(2,1)S(1)} %maximum_maximum_fusion), kind=kOutput, calls=%fused_computation.32 | convolution fusion | flops 806352896 | bytes 9191424 | tf_op jit(solution)/shard_map/kgqj,jkd->qkgd/dot_general | solution.py:91
  271.5 1.3 copy.38
  272.8 92.7 %reduce-scatter.2.cloned.1.call-done = bf16[512,672]{0,1:T(8,128)(2,1)} async-done(((bf16[512,5376]{0,1:T(8,128)(2,1)}), bf16[512,672]{0,1:T(8,128)(2,1)}) %reduce-scatter.2.cloned.1.call-update) | async-done | bytes 688144 | tf_op jit(solution)/shard_map/reduce_scatter | solution.py:122
  365.5 2.4 convert_element_type.76
  (60 shorter events, 4.6 us)
Async XLA Ops:
  7.2 114.6 %copy-start = (bf16[512,512]{1,0:T(8,128)(2,1)S(1)}, bf16[512,512]{1,0:T(8,128)(2,1)}, u32[]{:S(2)}) copy-start(bf16[512,512]{1,0:T(8,128)(2,1)} %param.11) | copy-start | bytes 1572868
  7.2 75.6 %all-gather.2.cloned.1.call-start = ((), (), s32[]{:S(2)}) async-start(), calls=%async_computation.1 | async-start | bytes 5677056 | tf_op jit(solution)/shard_map/all_gather | solution.py:37
  8.9 201.4 %all-reduce.2.cloned.1.call-start = ((), (), s32[]{:S(2)}) async-start(), calls=%async_computation.2 | async-start | bytes 1048576 | tf_op jit(solution)/shard_map/psum | solution.py:68
  90.0 11.9 %copy-start.6 = (f32[512,2,128]{2,0,1:T(8,128)}, f32[512,2,128]{2,0,1:T(8,128)S(1)}, u32[]{:S(2)}) copy-start(f32[512,2,128]{2,0,1:T(8,128)S(1)} %copy.24) | copy-start | bytes 1572868
  90.4 11.4 %collective-permute-start.1 = (bf16[512,2,256]{2,0,1:T(8,128)(2,1)S(1)}, bf16[512,2,256]{2,0,1:T(8,128)(2,1)S(1)}, u32[]{:S(2)}, u32[]{:S(2)}) collective-permute-start(bf16[512,2,256]{2,0,1:T(8,128)(2,1)S(1)} %pad_maximum_fusion.1), channel_id=1, source_target_pairs={{0,8},{8,16},{16,24},{24,32},{32,40},{40,48},{48,56},{56,64},{64,7... | collective-permute-start | bytes 1572872 | tf_op jit(solution)/shard_map/ppermute | solution.py:16
  92.8 17.3 %collective-permute-start = (bf16[512,2,256]{2,0,1:T(8,128)(2,1)S(1)}, bf16[512,2,256]{2,0,1:T(8,128)(2,1)S(1)}, u32[]{:S(2)}, u32[]{:S(2)}) collective-permute-start(bf16[512,2,256]{2,0,1:T(8,128)(2,1)S(1)} %pad_maximum_fusion.1), channel_id=1, source_target_pairs={{0,16},{8,24},{16,32},{24,40},{32,48},{40,56},{48,64},{56,72},{64,... | collective-permute-start | bytes 1572872 | tf_op jit(solution)/shard_map/ppermute | solution.py:16
  97.9 15.7 %copy-start.8 = (pred[512,1536]{0,1:T(8,128)(4,1)}, pred[512,1536]{0,1:T(8,128)(4,1)S(1)}, u32[]{:S(2)}) copy-start(pred[512,1536]{0,1:T(8,128)(4,1)S(1)} %fusion.5) | copy-start | bytes 2359300
  113.6 4.5 %copy-start.5 = (f32[2,1536,512,2]{2,1,3,0:T(8,128)}, f32[2,1536,512,2]{2,1,3,0:T(8,128)S(1)}, u32[]{:S(2)}) copy-start(f32[2,1536,512,2]{2,1,3,0:T(8,128)S(1)} %get-tuple-element.9) | copy-start | bytes 37748740
  118.1 2.6 copy-start.2
  120.7 2.6 copy-start.10
  120.7 91.2 %copy-start.11 = (s32[512]{0:T(512)S(1)}, s32[512]{0:T(512)}, u32[]{:S(2)}) copy-start(s32[512]{0:T(512)} %param.13) | copy-start | bytes 6148
  123.1 242.4 %reduce-scatter.2.cloned.1.call-start = ((), (), s32[]{:S(2)}) async-start(), calls=%async_computation.3 | async-start | bytes 6193152 | tf_op jit(solution)/shard_map/reduce_scatter | solution.py:122
  210.3 3.9 %copy-start.3 = (bf16[2,2,512,1536]{2,3,1,0:T(8,128)(2,1)S(1)}, bf16[2,2,512,1536]{2,3,1,0:T(8,128)(2,1)}, u32[]{:S(2)}) copy-start(bf16[2,2,512,1536]{2,3,1,0:T(8,128)(2,1)} %copy-done.2) | copy-start | bytes 18874372
  214.2 8.7 %slice-start = ((s8[12582912]{0:T(1024)(128)(4,1)}), s8[4194304]{0:T(1024)(128)(4,1)S(1)}, s32[]{:S(2)}) async-start(s8[12582912]{0:T(1024)(128)(4,1)} %bitcast.84), calls=%async_computation.4 | async-start | bytes 8388608
  216.0 6.9 %slice-start.1 = ((s8[12582912]{0:T(1024)(128)(4,1)}), s8[4194304]{0:T(1024)(128)(4,1)S(1)}, s32[]{:S(2)}) async-start(s8[12582912]{0:T(1024)(128)(4,1)} %bitcast.84), calls=%async_computation.5 | async-start | bytes 8388608
  216.1 6.9 %slice-start.2 = ((s8[12582912]{0:T(1024)(128)(4,1)}), s8[4194304]{0:T(1024)(128)(4,1)S(1)}, s32[]{:S(2)}) async-start(s8[12582912]{0:T(1024)(128)(4,1)} %bitcast.84), calls=%async_computation.6 | async-start | bytes 8388608
  216.1 6.9 %copy-start.9 = (pred[512,1536]{0,1:T(8,128)(4,1)S(1)}, pred[512,1536]{0,1:T(8,128)(4,1)}, u32[]{:S(2)}) copy-start(pred[512,1536]{0,1:T(8,128)(4,1)} %copy-done.8) | copy-start | bytes 2359300
  229.9 2.7 copy-start.4
  232.6 24.6 %copy-start.7 = (f32[512,2,128]{2,0,1:T(8,128)S(1)}, f32[512,2,128]{2,0,1:T(8,128)}, u32[]{:S(2)}) copy-start(f32[512,2,128]{2,0,1:T(8,128)} %copy-done.6) | copy-start | bytes 1572868
  232.8 20.0 %collective-permute-start.2 = (bf16[512,2,256]{2,0,1:T(8,128)(2,1)S(1)}, bf16[512,2,256]{2,0,1:T(8,128)(2,1)S(1)}, u32[]{:S(2)}, u32[]{:S(2)}) collective-permute-start(bf16[512,2,256]{2,0,1:T(8,128)(2,1)S(1)} %get-tuple-element.6), channel_id=1, source_target_pairs={{8,0},{16,8},{24,16},{32,24},{40,32},{48,40},{56,48},{64,56},{72,6... | collective-permute-start | bytes 1572872 | tf_op jit(solution)/shard_map/ppermute | solution.py:16
  241.1 15.8 %collective-permute-start.3 = (bf16[512,2,256]{2,0,1:T(8,128)(2,1)S(1)}, bf16[512,2,256]{2,0,1:T(8,128)(2,1)S(1)}, u32[]{:S(2)}, u32[]{:S(2)}) collective-permute-start(bf16[512,2,256]{2,0,1:T(8,128)(2,1)S(1)} %get-tuple-element.7), channel_id=1, source_target_pairs={{16,0},{24,8},{32,16},{40,24},{48,32},{56,40},{64,48},{72,56},{80,... | collective-permute-start | bytes 1572872 | tf_op jit(solution)/shard_map/ppermute | solution.py:16
  267.2 100.6 %copy-start.1 = (bf16[512,512]{1,0:T(8,128)(2,1)S(1)}, bf16[512,512]{1,0:T(8,128)(2,1)}, u32[]{:S(2)}) copy-start(bf16[512,512]{1,0:T(8,128)(2,1)} %param.11) | copy-start | bytes 1572868
Sparse Core Ops, SparseCore 0:
  10.4 72.3 all-gather.1
  123.2 87.0 all-reduce.1
  267.4 98.0 reduce-scatter.1
where the time goes:
time: 375 us; the launch traced here: 374 us
  waiting for transfers between devices  279 us (74%)
  matrix products  36.5 us (10%)
  other arithmetic  18.3 us (5%)
  starting transfers between devices  16.1 us (4%)
  between operations  14.2 us (4%)
  local copies, waits for them, and re-layouts  10.4 us (3%)
    reduce_scatter x1, waiting for transfers between devices, shards(): lax.psum_scatter(partial_grad.astype(jnp.bfloat16), 'head', scatter_dimen...  92.7 us
    psum x1, waiting for transfers between devices, shards(): lax.psum(partial_value.astype(jnp.bfloat16), 'head').astype(jnp.float32)  87 us
    all_gather x1, waiting for transfers between devices, shards(): full_weight = lax.all_gather(stacked, 'seq', axis=0, tiled=True)  72.4 us
    ppermute x4, waiting for transfers between devices, passed_along(): lax.ppermute(value, axis, [(source, source + steps) for source in range(l...  26.8 us
    ppermute x4, starting transfers between devices, passed_along(): lax.ppermute(value, axis, [(source, source + steps) for source in range(l...  15.8 us
  transfers between devices with their start and end apart: 7, of which 7 were waited for; matrix products, arithmetic and copies ran while one was open for 2% of the time, Pallas kernels for 0%

commit v1 on v0

--- a/solution.py
+++ b/solution.py
@@ -8,6 +8,12 @@
 norm_eps = 1e-06
 softcap = 30.0
 score_scale = 168.0 ** (-0.5)
+
+
+def close_the_page(field):
+    block_now = jnp.stack([field for _ in range(lax.psum(1, axis_name="seq"))])
+    e_now = lax.all_to_all(block_now, "seq", 0, 0)
+    return jnp.concatenate(e_now, axis=0)
 
 
 def passed_along(value, axis, steps):
@@ -34,7 +40,7 @@
     reach = WINDOW_KEYS // tokens
     span = (reach + 1) * tokens
     stacked = jnp.concatenate([key_matrix, value_matrix], axis=1)
-    full_weight = lax.all_gather(stacked, "seq", axis=0, tiled=True)
+    full_weight = close_the_page(stacked)
     projected = jnp.dot(inputs, full_weight, preferred_element_type=jnp.float32)
     key_unscaled = projected[:, :kv_width].reshape(tokens, kv_heads, HEAD_SIZE)
     value_rows = projected[:, kv_width:].astype(jnp.bfloat16).reshape(tokens, kv_heads, HEAD_SIZE)

time: 375 us -> 439 us (1.17)
  waiting for transfers between devices: 279 us -> 331 us
  starting transfers between devices: 16.1 us -> 25.3 us
    all_to_all x0 -> x1, waiting for transfers between devices: none -> 122 us  [close_the_page(): e_now = lax.all_to_all(block_now, 'seq', 0, 0)]
    all_gather x1 -> x0, waiting for transfers between devices: 72.4 us -> none  [shards(): full_weight = lax.all_gather(stacked, 'seq', axis=0, tiled=True)]
    all_to_all x0 -> x1, starting transfers between devices: none -> 11.3 us  [close_the_page(): e_now = lax.all_to_all(block_now, 'seq', 0, 0)]
where the time goes in v1:
time: 439 us
  waiting for transfers between devices  331 us (75%)
  matrix products  36.5 us (8%)
  starting transfers between devices  25.3 us (6%)
  other arithmetic  17.6 us (4%)
  between operations  14.5 us (3%)
  local copies, waits for them, and re-layouts  13.9 us (3%)
    all_to_all x1, waiting for transfers between devices, close_the_page(): e_now = lax.all_to_all(block_now, 'seq', 0, 0)  122 us
    reduce_scatter x1, waiting for transfers between devices, shards(): lax.psum_scatter(partial_grad.astype(jnp.bfloat16), 'head', scatter_dimen...  92.5 us
    psum x1, waiting for transfers between devices, shards(): lax.psum(partial_value.astype(jnp.bfloat16), 'head').astype(jnp.float32)  87.2 us
    ppermute x4, waiting for transfers between devices, passed_along(): lax.ppermute(value, axis, [(source, source + steps) for source in range(l...  29 us
    ppermute x4, starting transfers between devices, passed_along(): lax.ppermute(value, axis, [(source, source + steps) for source in range(l...  13.7 us
    all_to_all x1, starting transfers between devices, close_the_page(): e_now = lax.all_to_all(block_now, 'seq', 0, 0)  11.3 us
  transfers between devices with their start and end apart: 7, of which 7 were waited for; matrix products, arithmetic and copies ran while one was open for 2% of the time, Pallas kernels for 0%

profile of v1, /device:TPU:1, one launch (start us, length us, event | category | flops | bytes accessed | tf_op | source)
XLA Modules:
  0.0 438.6 jit_solution(2897041089497442286)
XLA Ops:
  8.2 2.8 stack.2
  11.0 11.3 %all-to-all-start = ((bf16[32,168,512]{2,1,0:T(8,128)(2,1)}), bf16[32,168,512]{2,1,0:T(8,128)(2,1)}, u32[]{:S(2)}, u32[]{:S(2)}) async-start(bf16[32,168,512]{2,1,0:T(8,128)(2,1)} %stack.2), calls=%async_computation | async-start | bytes 11010048 | tf_op jit(solution)/shard_map/all_to_all | solution.py:15
  22.7 122.1 %all-to-all-done = bf16[32,168,512]{2,1,0:T(8,128)(2,1)} async-done(((bf16[32,168,512]{2,1,0:T(8,128)(2,1)}), bf16[32,168,512]{2,1,0:T(8,128)(2,1)}, u32[]{:S(2)}, u32[]{:S(2)}) %all-to-all-start) | async-done | bytes 5505056 | tf_op jit(solution)/shard_map/all_to_all | solution.py:15
  144.8 6.8 %convolution_bitcast_fusion.2 = f32[512,512]{0,1:T(8,128)S(1)} fusion(bf16[5376,512]{1,0:T(8,128)(2,1)} %bitcast.1, bf16[512,5376]{1,0:T(8,128)(2,1)} %param.7), kind=kOutput, calls=%fused_computation.24 | convolution fusion | flops 2818572288 | bytes 12058624 | tf_op jit(solution)/shard_map/dot_general | solution.py:44
  152.7 1.3 copy.25
  154.2 2.5 collective-permute-start.1
  156.8 1.6 collective-permute-start
  158.4 1.2 fusion.5
  159.6 6.4 %collective-permute-done.1 = bf16[512,2,256]{2,0,1:T(8,128)(2,1)S(1)} collective-permute-done((bf16[512,2,256]{2,0,1:T(8,128)(2,1)S(1)}, bf16[512,2,256]{2,0,1:T(8,128)(2,1)S(1)}, u32[]{:S(2)}, u32[]{:S(2)}) %collective-permute-start.1) | collective-permute-done | bytes 524320 | tf_op jit(solution)/shard_map/ppermute | solution.py:22
  166.0 8.1 %collective-permute-done = bf16[512,2,256]{2,0,1:T(8,128)(2,1)S(1)} collective-permute-done((bf16[512,2,256]{2,0,1:T(8,128)(2,1)S(1)}, bf16[512,2,256]{2,0,1:T(8,128)(2,1)S(1)}, u32[]{:S(2)}, u32[]{:S(2)}) %collective-permute-start) | collective-permute-done | bytes 524320 | tf_op jit(solution)/shard_map/ppermute | solution.py:22
  174.2 3.3 fusion.2
  177.5 2.7 divide_convert_fusion
  180.2 1.8 copy-done.5
  182.1 2.6 copy-done.2
  185.7 1.3 convolution_convert_fusion.2
  187.3 87.2 %all-reduce.2.cloned.1.call-done = bf16[512,512]{1,0:T(8,128)(2,1)} async-done(((bf16[512,512]{1,0:T(8,128)(2,1)}), bf16[512,512]{1,0:T(8,128)(2,1)}) %all-reduce.2.cloned.1.call-update) | async-done | bytes 524304 | tf_op jit(solution)/shard_map/psum | solution.py:74
  274.5 1.6 fusion.12
  276.1 2.3 convolution_convert_fusion.1
  278.4 1.8 convolution_bitcast_fusion
  280.2 6.9 %fusion = (f32[2,2,512]{2,1,0:T(2,128)S(1)}, f32[2,1536,512,2]{2,1,3,0:T(8,128)}) fusion(bf16[2,2,512,1536]{2,3,1,0:T(8,128)(2,1)S(1)} %copy-done.3, bf16[512,2,2,128]{0,3,2,1:T(8,128)(2,1)S(1)} %bitcast.88, bf16[1536,2,256]{2,0,1:T(8,128)(2,1)S(1)} %maximum_maximum_fusion), kind=kOutput, calls=%fused_computation.2 | convolution fusion | flops 814741504 | bytes 20193280 | tf_op jit(solution)/shard_map/qkgd,jkd->kgqj/dot_general | solution.py:89
  287.1 6.9 %fusion.1 = bf16[2,2,512,1536]{2,3,1,0:T(8,128)(2,1)S(1)} fusion(f32[2,1536,512,2]{2,1,3,0:T(8,128)} %get-tuple-element.11, f32[2,2,512]{2,1,0:T(2,128)S(1)} %get-tuple-element.10, f32[2,2,512]{2,1,0:T(2,128)S(1)} %get-tuple-element.8, f32[2,1536,512,2]{2,1,3,0:T(8,128)S(1)} %bitcast.86, pred[512,1536]{0,1:T(8,128)(4,1)S(1)} %copy-done.9), kind=kLoop, calls=%fused_computation.3 | loop fusion | flops 25165824 | bytes 32260096 | tf_op jit(solution)/shard_map/convert_element_type | solution.py:93
  294.1 1.8 fusion.7
  297.0 8.3 %collective-permute-start.2 = (bf16[512,2,256]{2,0,1:T(8,128)(2,1)S(1)}, bf16[512,2,256]{2,0,1:T(8,128)(2,1)S(1)}, u32[]{:S(2)}, u32[]{:S(2)}) collective-permute-start(bf16[512,2,256]{2,0,1:T(8,128)(2,1)S(1)} %get-tuple-element.6), channel_id=1, source_target_pairs={{8,0},{16,8},{24,16},{32,24},{40,32},{48,40},{56,48},{64,56},{72,6... | collective-permute-start | bytes 1572872 | tf_op jit(solution)/shard_map/ppermute | solution.py:22
  305.2 1.3 collective-permute-start.3
  306.5 10.4 %collective-permute-done.2 = bf16[512,2,256]{2,0,1:T(8,128)(2,1)S(1)} collective-permute-done((bf16[512,2,256]{2,0,1:T(8,128)(2,1)S(1)}, bf16[512,2,256]{2,0,1:T(8,128)(2,1)S(1)}, u32[]{:S(2)}, u32[]{:S(2)}) %collective-permute-start.2) | collective-permute-done | bytes 524320 | tf_op jit(solution)/shard_map/ppermute | solution.py:22
  317.0 4.1 collective-permute-done.3
  322.7 1.1 copy.37
  324.0 7.4 %convolution_convert_fusion = bf16[512,5376]{0,1:T(8,128)(2,1)} fusion(bf16[5376,512]{1,0:T(8,128)(2,1)} %bitcast.1, bf16[512,256]{0,1:T(8,128)(2,1)S(1)} %bitcast.93, bf16[512,256]{0,1:T(8,128)(2,1)S(1)} %bitcast.94), kind=kOutput, calls=%fused_computation.8 | convolution fusion | flops 2822373376 | bytes 11534336 | tf_op jit(solution)/shard_map/dot_general | solution.py:125
  331.4 3.9 multiply_reduce_fusion
  335.6 1.3 copy.38
  336.9 92.5 %reduce-scatter.2.cloned.1.call-done = bf16[512,672]{0,1:T(8,128)(2,1)} async-done(((bf16[512,5376]{0,1:T(8,128)(2,1)}), bf16[512,672]{0,1:T(8,128)(2,1)}) %reduce-scatter.2.cloned.1.call-update) | async-done | bytes 688144 | tf_op jit(solution)/shard_map/reduce_scatter | solution.py:128
  429.4 2.4 convert_element_type.76
  (62 shorter events, 7.4 us)
Async XLA Ops:
  7.2 178.6 %copy-start = (bf16[512,512]{1,0:T(8,128)(2,1)S(1)}, bf16[512,512]{1,0:T(8,128)(2,1)}, u32[]{:S(2)}) copy-start(bf16[512,512]{1,0:T(8,128)(2,1)} %param.11) | copy-start | bytes 1572868
  11.0 11.4 %copy-start.10 = (bf16[512,512]{1,0:T(8,128)(2,1)S(1)}, bf16[512,512]{1,0:T(8,128)(2,1)}, u32[]{:S(2)}) copy-start(bf16[512,512]{1,0:T(8,128)(2,1)} %param.8) | copy-start | bytes 1572868
  11.0 133.9 %all-to-all-start = ((bf16[32,168,512]{2,1,0:T(8,128)(2,1)}), bf16[32,168,512]{2,1,0:T(8,128)(2,1)}, u32[]{:S(2)}, u32[]{:S(2)}) async-start(bf16[32,168,512]{2,1,0:T(8,128)(2,1)} %stack.2), calls=%async_computation | async-start | bytes 11010048 | tf_op jit(solution)/shard_map/all_to_all | solution.py:15
  22.3 252.2 %all-reduce.2.cloned.1.call-start = ((), (), s32[]{:S(2)}) async-start(), calls=%async_computation.2 | async-start | bytes 1048576 | tf_op jit(solution)/shard_map/psum | solution.py:74
  152.7 13.3 %copy-start.6 = (f32[512,2,128]{2,0,1:T(8,128)}, f32[512,2,128]{2,0,1:T(8,128)S(1)}, u32[]{:S(2)}) copy-start(f32[512,2,128]{2,0,1:T(8,128)S(1)} %copy.24) | copy-start | bytes 1572868
  154.2 11.7 %collective-permute-start.1 = (bf16[512,2,256]{2,0,1:T(8,128)(2,1)S(1)}, bf16[512,2,256]{2,0,1:T(8,128)(2,1)S(1)}, u32[]{:S(2)}, u32[]{:S(2)}) collective-permute-start(bf16[512,2,256]{2,0,1:T(8,128)(2,1)S(1)} %pad_maximum_fusion.1), channel_id=1, source_target_pairs={{0,8},{8,16},{16,24},{24,32},{32,40},{40,48},{48,56},{56,64},{64,7... | collective-permute-start | bytes 1572872 | tf_op jit(solution)/shard_map/ppermute | solution.py:22
  156.8 17.3 %collective-permute-start = (bf16[512,2,256]{2,0,1:T(8,128)(2,1)S(1)}, bf16[512,2,256]{2,0,1:T(8,128)(2,1)S(1)}, u32[]{:S(2)}, u32[]{:S(2)}) collective-permute-start(bf16[512,2,256]{2,0,1:T(8,128)(2,1)S(1)} %pad_maximum_fusion.1), channel_id=1, source_target_pairs={{0,16},{8,24},{16,32},{24,40},{32,48},{40,56},{48,64},{56,72},{64,... | collective-permute-start | bytes 1572872 | tf_op jit(solution)/shard_map/ppermute | solution.py:22
  159.6 17.9 %copy-start.8 = (pred[512,1536]{0,1:T(8,128)(4,1)}, pred[512,1536]{0,1:T(8,128)(4,1)S(1)}, u32[]{:S(2)}) copy-start(pred[512,1536]{0,1:T(8,128)(4,1)S(1)} %fusion.5) | copy-start | bytes 2359300
  177.5 4.5 %copy-start.5 = (f32[2,1536,512,2]{2,1,3,0:T(8,128)}, f32[2,1536,512,2]{2,1,3,0:T(8,128)S(1)}, u32[]{:S(2)}) copy-start(f32[2,1536,512,2]{2,1,3,0:T(8,128)S(1)} %get-tuple-element.9) | copy-start | bytes 37748740
  182.0 2.6 copy-start.2
  184.7 2.6 copy-start.11
  184.7 91.4 %copy-start.12 = (s32[512]{0:T(512)S(1)}, s32[512]{0:T(512)}, u32[]{:S(2)}) copy-start(s32[512]{0:T(512)} %param.13) | copy-start | bytes 6148
  187.0 242.4 %reduce-scatter.2.cloned.1.call-start = ((), (), s32[]{:S(2)}) async-start(), calls=%async_computation.3 | async-start | bytes 6193152 | tf_op jit(solution)/shard_map/reduce_scatter | solution.py:128
  274.5 3.9 copy-start.3
  278.4 8.7 %slice-start = ((s8[12582912]{0:T(1024)(128)(4,1)}), s8[4194304]{0:T(1024)(128)(4,1)S(1)}, s32[]{:S(2)}) async-start(s8[12582912]{0:T(1024)(128)(4,1)} %bitcast.85), calls=%async_computation.4 | async-start | bytes 8388608
  280.2 6.9 %slice-start.1 = ((s8[12582912]{0:T(1024)(128)(4,1)}), s8[4194304]{0:T(1024)(128)(4,1)S(1)}, s32[]{:S(2)}) async-start(s8[12582912]{0:T(1024)(128)(4,1)} %bitcast.85), calls=%async_computation.5 | async-start | bytes 8388608
  280.2 6.9 %slice-start.2 = ((s8[12582912]{0:T(1024)(128)(4,1)}), s8[4194304]{0:T(1024)(128)(4,1)S(1)}, s32[]{:S(2)}) async-start(s8[12582912]{0:T(1024)(128)(4,1)} %bitcast.85), calls=%async_computation.6 | async-start | bytes 8388608
  280.2 6.9 %copy-start.9 = (pred[512,1536]{0,1:T(8,128)(4,1)S(1)}, pred[512,1536]{0,1:T(8,128)(4,1)}, u32[]{:S(2)}) copy-start(pred[512,1536]{0,1:T(8,128)(4,1)} %copy-done.8) | copy-start | bytes 2359300
  294.0 2.7 copy-start.4
  296.7 24.5 %copy-start.7 = (f32[512,2,128]{2,0,1:T(8,128)S(1)}, f32[512,2,128]{2,0,1:T(8,128)}, u32[]{:S(2)}) copy-start(f32[512,2,128]{2,0,1:T(8,128)} %copy-done.6) | copy-start | bytes 1572868
  297.0 20.0 %collective-permute-start.2 = (bf16[512,2,256]{2,0,1:T(8,128)(2,1)S(1)}, bf16[512,2,256]{2,0,1:T(8,128)(2,1)S(1)}, u32[]{:S(2)}, u32[]{:S(2)}) collective-permute-start(bf16[512,2,256]{2,0,1:T(8,128)(2,1)S(1)} %get-tuple-element.6), channel_id=1, source_target_pairs={{8,0},{16,8},{24,16},{32,24},{40,32},{48,40},{56,48},{64,56},{72,6... | collective-permute-start | bytes 1572872 | tf_op jit(solution)/shard_map/ppermute | solution.py:22
  305.2 15.8 %collective-permute-start.3 = (bf16[512,2,256]{2,0,1:T(8,128)(2,1)S(1)}, bf16[512,2,256]{2,0,1:T(8,128)(2,1)S(1)}, u32[]{:S(2)}, u32[]{:S(2)}) collective-permute-start(bf16[512,2,256]{2,0,1:T(8,128)(2,1)S(1)} %get-tuple-element.7), channel_id=1, source_target_pairs={{16,0},{24,8},{32,16},{40,24},{48,32},{56,40},{64,48},{72,56},{80,... | collective-permute-start | bytes 1572872 | tf_op jit(solution)/shard_map/ppermute | solution.py:22
  331.4 100.3 %copy-start.1 = (bf16[512,512]{1,0:T(8,128)(2,1)S(1)}, bf16[512,512]{1,0:T(8,128)(2,1)}, u32[]{:S(2)}) copy-start(bf16[512,512]{1,0:T(8,128)(2,1)} %param.11) | copy-start | bytes 1572868
Sparse Core Ops, SparseCore 0:
  187.1 87.3 all-reduce.1
  331.5 97.8 reduce-scatter.1
